TPU v7x, 32 devices: a whole 2x2x4 slice. The times are simulated.
32 devices in a mesh: dp: 8 (over z, x), mp: 4 (over y, core).
Axes of the slice: x: 2, y: 2, z: 4, core: 2. Of those that a mesh axis runs over, the one named last changes fastest.
Arguments:
- latent: bfloat16 [65536, 512], P('dp'), may hold values from -6 to 6
- actions: bfloat16 [6, 65536], P(None, 'dp'), may hold values from -1 to 1
- task_ids: int32 [65536], P('dp'), may hold values from 0 to 79
- action_masks: int32 [80, 6], replicated, may hold values 0 or 1
- next_latent: bfloat16 [65536, 512], P('dp', 'mp'), may hold values from 0 to 0.25
- reward_bins: int32 [65536], P('dp'), may hold values from 0 to 99
- reward_frac: float32 [65536], P('dp'), may hold values from 0 to 1
- task_embed: bfloat16 [80, 96], replicated, may hold values from -6 to 6
- dyn_w1: bfloat16 [614, 1024], P(None, 'mp'), may hold values from -0.25 to 0.25
- dyn_b1: float32 [1024], P('mp'), may hold values from -3 to 3
- dyn_gain: float32 [1024], P('mp'), may hold values from 0.5 to 1.5
- dyn_shift: float32 [1024], P('mp'), may hold values from -2 to 2
- rew_w1: bfloat16 [614, 1024], P(None, 'mp'), may hold values from -0.25 to 0.25
- rew_b1: float32 [1024], P('mp'), may hold values from -3 to 3
- rew_gain: float32 [1024], P('mp'), may hold values from 0.5 to 1.5
- rew_shift: float32 [1024], P('mp'), may hold values from -2 to 2
- dyn_w2: bfloat16 [1024, 512], P('mp'), may hold values from -0.375 to 0.375
- dyn_b2: float32 [512], replicated, may hold values from -2 to 2
- rew_w2: bfloat16 [1024, 101], P('mp'), may hold values from -0.375 to 0.375
- rew_b2: float32 [101], replicated, may hold values from -2 to 2
Outputs:
- latents: bfloat16 [65536, 512], P('dp', 'mp')
- latent_grad: bfloat16 [65536, 512], P('dp', 'mp')
- losses: float32 [2], replicated
- grad_task_embed: float32 [80, 96], replicated
- grad_dyn_w1: float32 [614, 1024], P(None, 'mp')
- grad_dyn_b1: float32 [1024], P('mp')
- grad_dyn_gain: float32 [1024], P('mp')
- grad_dyn_shift: float32 [1024], P('mp')
- grad_rew_w1: float32 [614, 1024], P(None, 'mp')
- grad_rew_b1: float32 [1024], P('mp')
- grad_rew_gain: float32 [1024], P('mp')
- grad_rew_shift: float32 [1024], P('mp')
- grad_dyn_w2: float32 [1024, 512], P('mp')
- grad_dyn_b2: float32 [512], replicated
- grad_rew_w2: float32 [1024, 101], P('mp')
- grad_rew_b2: float32 [101], replicated
Inputs may be any that keep to these rules, and one draw needn't show every extreme that they name: The upper bin reward_bins + 1 is a valid bin.
All inputs are finite; a program needn't handle non-finite values.
Results may differ from a plain program's by a relative error of at most 0.024.
Values may be sent and summed in bfloat16 or wider, within the bound.
A program may use at most 192 MiB of HBM per device.

v0:
```python
import jax
import jax.numpy as jnp
from jax import lax
from jax.sharding import PartitionSpec as P

HID = 1024
GROUP = 8
CONS_COEF = 20.0
REW_COEF = 0.1


def mish_act(values):
    return values * jnp.tanh(jax.nn.softplus(values))


def contract(left, right, left_dim, right_dim):
    return lax.dot_general(
        left, right, (((left_dim,), (right_dim,)), ((), ())), preferred_element_type=jnp.float32
    )


def on_device(
    latent,
    actions,
    task_ids,
    action_masks,
    next_latent,
    reward_bins,
    reward_frac,
    task_embed,
    dyn_w1,
    dyn_b1,
    dyn_gain,
    dyn_shift,
    rew_w1,
    rew_b1,
    rew_gain,
    rew_shift,
    dyn_w2,
    dyn_b2,
    rew_w2,
    rew_b2,
):
    tok_rows = latent.shape[0]
    shard_width = dyn_w1.shape[1]
    share_width = next_latent.shape[1]
    n_model = lax.axis_size("mp")
    total_rows = tok_rows * lax.axis_size("dp")
    mp_index = lax.axis_index("mp")
    lat_width = latent.shape[1]
    act_width = actions.shape[0]
    onehot = (
        task_ids[:, None] == jnp.arange(task_embed.shape[0], dtype=jnp.int32)[None, :]
    ).astype(jnp.bfloat16)
    embedded = jnp.dot(onehot, task_embed, preferred_element_type=jnp.float32).astype(jnp.bfloat16)
    mask_cols = contract(action_masks.astype(jnp.bfloat16), onehot, 0, 1)
    masked = (actions.astype(jnp.float32) * mask_cols).astype(jnp.bfloat16)
    w_first = jnp.concatenate([dyn_w1, rew_w1], axis=1)
    w_lat = w_first[:lat_width]
    w_act = w_first[lat_width : lat_width + act_width]
    w_task = w_first[lat_width + act_width :]
    bias_pair = jnp.concatenate([dyn_b1, rew_b1])
    pre_act = (
        jnp.dot(latent, w_lat, preferred_element_type=jnp.float32)
        + contract(masked, w_act, 0, 0)
        + jnp.dot(embedded, w_task, preferred_element_type=jnp.float32)
        + bias_pair
    )
    pre_act = pre_act.reshape(tok_rows, 2, shard_width)
    first_sum, second_sum = lax.psum(
        (jnp.sum(pre_act, axis=2).T, jnp.sum(pre_act * pre_act, axis=2).T), "mp"
    )
    average = first_sum / HID
    variance = second_sum / HID - average * average
    inv_std = lax.rsqrt(variance + 1e-05).T[:, :, None]
    normalized = (pre_act - average.T[:, :, None]) * inv_std
    gain_pair = jnp.stack([dyn_gain, rew_gain])
    shift_pair = jnp.stack([dyn_shift, rew_shift])
    normed = normalized * gain_pair + shift_pair
    hidden = mish_act(normed).astype(jnp.bfloat16)
    hidden_dyn = hidden[:, 0]
    hidden_rew = hidden[:, 1]
    lat_part = jnp.dot(hidden_dyn, dyn_w2, preferred_element_type=jnp.float32).astype(jnp.bfloat16)
    lat_share = lax.psum_scatter(lat_part, "mp", scatter_dimension=1, tiled=True).astype(
        jnp.float32
    )
    lat_share = lat_share + lax.dynamic_slice_in_dim(dyn_b2, mp_index * share_width, share_width)
    logit_part = jnp.dot(hidden_rew, rew_w2, preferred_element_type=jnp.float32)
    logits = lax.psum(logit_part, "mp") + rew_b2
    groups = lat_share.reshape(tok_rows, share_width // GROUP, GROUP)
    simplex = jax.nn.softmax(groups, axis=-1)
    latents_out = simplex.reshape(tok_rows, share_width)
    lat_error = latents_out - next_latent.astype(jnp.float32)
    cons_part = jnp.sum(lat_error * lat_error)
    log_probs = jax.nn.log_softmax(logits, axis=-1)
    bin_iota = jnp.arange(logits.shape[1], dtype=jnp.int32)[None, :]
    target = jnp.where(bin_iota == reward_bins[:, None], 1.0 - reward_frac[:, None], 0.0)
    target = target + jnp.where(bin_iota == reward_bins[:, None] + 1, reward_frac[:, None], 0.0)
    rew_part = -jnp.sum(target * log_probs) / n_model
    d_groups = (2.0 * CONS_COEF / total_rows * lat_error).reshape(groups.shape)
    d_lat = simplex * (d_groups - jnp.sum(simplex * d_groups, axis=-1, keepdims=True))
    d_share = d_lat.reshape(tok_rows, share_width).astype(jnp.bfloat16)
    d_full = lax.all_gather(d_share, "mp", axis=1, tiled=True)
    d_logits = (REW_COEF / total_rows * (jnp.exp(log_probs) - target)).astype(jnp.bfloat16)
    grad_w2_dyn = contract(hidden_dyn, d_full, 0, 0)
    grad_b2_dyn = jnp.sum(d_full.astype(jnp.float32), axis=0)
    grad_w2_rew = contract(hidden_rew, d_logits, 0, 0)
    grad_b2_rew = jnp.sum(d_logits.astype(jnp.float32), axis=0)
    head_grads = (grad_w2_dyn, grad_b2_dyn, grad_w2_rew, grad_b2_rew)
    d_hid_dyn = contract(d_full, dyn_w2, 1, 1)
    d_hid_rew = contract(d_logits, rew_w2, 1, 1)
    d_hidden = jnp.stack([d_hid_dyn, d_hid_rew], axis=1)
    unused_value, mish_back = jax.vjp(mish_act, normed)
    d_normed = mish_back(d_hidden)[0]
    grad_gain = jnp.sum(d_normed * normalized, axis=0)
    grad_shift = jnp.sum(d_normed, axis=0)
    d_unit = d_normed * gain_pair
    back_first, back_second = lax.psum(
        (jnp.sum(d_unit, axis=2).T, jnp.sum(d_unit * normalized, axis=2).T), "mp"
    )
    d_pre = inv_std * (
        d_unit - (back_first.T / HID)[:, :, None] - normalized * (back_second.T / HID)[:, :, None]
    )
    d_pre = d_pre.reshape(tok_rows, 2 * shard_width).astype(jnp.bfloat16)
    grad_b1 = jnp.sum(d_pre.astype(jnp.float32), axis=0)
    grad_w_lat = contract(latent, d_pre, 0, 0)
    grad_w_act = jnp.dot(masked, d_pre, preferred_element_type=jnp.float32)
    task_sums = contract(onehot, d_pre, 0, 0)
    grad_w_task = jnp.dot(
        task_embed.astype(jnp.float32).T, task_sums, precision=lax.Precision.HIGHEST
    )
    embed_part = jnp.dot(task_sums, w_task.astype(jnp.float32).T, precision=lax.Precision.HIGHEST)
    grad_w1 = jnp.concatenate([grad_w_lat, grad_w_act, grad_w_task], axis=0)
    input_part = contract(d_pre, w_lat, 1, 1).astype(jnp.bfloat16)
    input_share = lax.psum_scatter(input_part, "mp", scatter_dimension=1, tiled=True).astype(
        jnp.float32
    )
    latent_grad = (input_share * total_rows).astype(jnp.bfloat16)
    cons_sum, rew_sum, grad_embed = lax.psum((cons_part, rew_part, embed_part), ("dp", "mp"))
    losses = jnp.stack([cons_sum, rew_sum]) / total_rows
    summed = lax.psum(
        (
            grad_w1,
            grad_b1,
            grad_gain,
            grad_shift,
            head_grads[0],
            head_grads[1],
            head_grads[2],
            head_grads[3],
        ),
        "dp",
    )
    grad_w1, grad_b1, grad_gain, grad_shift = (summed[0], summed[1], summed[2], summed[3])
    head_grads = (summed[4], summed[5], summed[6], summed[7])
    return (
        latents_out.astype(jnp.bfloat16),
        latent_grad,
        losses,
        grad_embed,
        grad_w1[:, :shard_width],
        grad_b1[:shard_width],
        grad_gain[0],
        grad_shift[0],
        grad_w1[:, shard_width:],
        grad_b1[shard_width:],
        grad_gain[1],
        grad_shift[1],
        head_grads[0],
        head_grads[1],
        head_grads[2],
        head_grads[3],
    )


def solution(mesh):
    return jax.shard_map(
        on_device,
        mesh=mesh,
        in_specs=(
            P("dp", None),
            P(None, "dp"),
            P("dp"),
            P(),
            P("dp", "mp"),
            P("dp"),
            P("dp"),
            P(),
            P(None, "mp"),
            P("mp"),
            P("mp"),
            P("mp"),
            P(None, "mp"),
            P("mp"),
            P("mp"),
            P("mp"),
            P("mp", None),
            P(),
            P("mp", None),
            P(),
        ),
        out_specs=(
            P("dp", "mp"),
            P("dp", "mp"),
            P(),
            P(),
            P(None, "mp"),
            P("mp"),
            P("mp"),
            P("mp"),
            P(None, "mp"),
            P("mp"),
            P("mp"),
            P("mp"),
            P("mp", None),
            P(),
            P("mp", None),
            P(),
        ),
        check_vma=False,
    )
```

profile of v0, /device:TPU:0, one launch (start us, length us, event | category | flops | bytes accessed | tf_op | source)
XLA Modules:
  0.0 630.1 jit_solution(13819635788461500749)
XLA Ops:
  10.0 11.8 %fusion.39 = f32[512,8192]{1,0:T(8,128)} fusion(bf16[8192,512]{1,0:T(8,128)(2,1)} %param.20, bf16[614,512]{1,0:T(8,128)(2,1)S(1)} %constant_dynamic-update-slice_fusion), kind=kOutput, calls=%fused_computation.95 | convolution fusion | flops 4294967296 | bytes 25690112 | tf_op jit(solution)/shard_map/dot_general | solution.py:64
  21.8 7.3 %fusion.33 = f32[8192,512]{0,1:T(8,128)} fusion(bf16[80,96]{1,0:T(8,128)(2,1)S(1)} %copy-done.21, s32[8192]{0:T(1024)S(1)} %copy-done.16, bf16[614,512]{1,0:T(8,128)(2,1)S(1)} %constant_dynamic-update-slice_fusion), kind=kOutput, calls=%fused_computation.87 | convolution fusion | flops 932577280 | bytes 16928768 | tf_op jit(solution)/shard_map/dot_general | solution.py:66
  29.7 19.8 %bitcast_reduce_fusion = (f32[8192,2]{0,1:T(2,128)}, f32[8192,2]{0,1:T(2,128)}, f32[8192,512]{0,1:T(8,128)}) fusion(f32[512]{0:T(512)S(1)} %pad_maximum_fusion.2, f32[8192,512]{0,1:T(8,128)} %fusion.33, bf16[6,8192]{1,0:T(8,128)(2,1)S(1)} %fusion.23, bf16[614,512]{1,0:T(8,128)(2,1)S(1)} %constant_dynamic-update-slice_fusion, f32[512,8192]{1,0:T(8,128)} %fusion.39), kind=kOutput, calls=%fused_computation.29 | convolution fusion | flops 75464704 | bytes 50604032 | tf_op jit(solution)/shard_map/dot_general | solution.py:17
  49.9 34.0 %all-reduce.16.cloned.1.call-done = (f32[2,8192]{1,0:T(2,128)}, f32[2,8192]{1,0:T(2,128)}) async-done(((f32[2,8192]{1,0:T(2,128)}, f32[2,8192]{1,0:T(2,128)}), (f32[2,8192]{1,0:T(2,128)}, f32[2,8192]{1,0:T(2,128)})) %all-reduce.16.cloned.1.call-update) | async-done | bytes 131088 | tf_op jit(solution)/shard_map/psum | solution.py:70
  84.9 14.7 %fusion.17 = bf16[8192,2,256]{0,2,1:T(8,128)(2,1)S(1)} fusion(f32[8192,512]{0,1:T(8,128)} %get-tuple-element.93, f32[2,256]{1,0:T(2,128)S(1)} %get-tuple-element.92, f32[2,256]{1,0:T(2,128)S(1)} %get-tuple-element.94, f32[8192,2]{0,1:T(2,128)S(1)} %get-tuple-element.82, f32[8192,2]{0,1:T(2,128)S(1)} %get-tuple-element.81), kind=kLoop, calls=%fused_computation.41 | loop fusion | flops 50331648 | bytes 25300992 | tf_op jit(solution)/shard_map/convert_element_type | solution.py:80
  102.8 5.6 convolution_convert_fusion.1
  108.4 12.1 %copy.47 = bf16[8192,512]{0,1:T(8,128)(2,1)} copy(bf16[8192,512]{1,0:T(8,128)(2,1)} %convolution_convert_fusion.1) | data formatting | bytes 16777216
  130.2 62.2 %reduce-scatter.7.cloned.1.call-done = bf16[128,8192]{1,0:T(8,128)(2,1)} async-done(((bf16[512,8192]{1,0:T(8,128)(2,1)}), bf16[128,8192]{1,0:T(8,128)(2,1)}) %reduce-scatter.7.cloned.1.call-update) | async-done | bytes 2097168
  198.8 7.2 %fusion.21 = bf16[8192,128]{0,1:T(8,128)(2,1)} fusion(bf16[8192,128]{0,1:T(8,128)(2,1)S(1)} %copy.45, bf16[128,8192]{1,0:T(8,128)(2,1)} %reduce-scatter.7.cloned.1.call-done, f32[8192,16]{0,1:T(8,128)S(1)} %fusion.26, f32[8192,16]{0,1:T(8,128)S(1)} %bitcast_reduce_fusion.1, f32[128]{0:T(128)} %copy-done.24), kind=kOutput, calls=%fused_computation.52 | output fusion | flops 21102600 | bytes 7340544 | tf_op jit(solution)/shard_map/sub | solution.py:101
  208.0 59.5 %all-reduce.10.cloned.1.call-done = f32[8192,101]{0,1:T(8,128)} async-done(((f32[8192,101]{0,1:T(8,128)}), f32[8192,101]{0,1:T(8,128)}) %all-reduce.10.cloned.1.call-update) | async-done | bytes 3309584 | tf_op jit(solution)/shard_map/psum | solution.py:89
  276.7 5.9 convolution_bitcast_fusion.1
  284.7 43.2 %all-gather.2.cloned.1.call-done = bf16[8192,512]{0,1:T(8,128)(2,1)} async-done(((bf16[8192,128]{0,1:T(8,128)(2,1)}), bf16[8192,512]{0,1:T(8,128)(2,1)}) %all-gather.2.cloned.1.call-update) | async-done | bytes 8388624 | tf_op jit(solution)/shard_map/all_gather | solution.py:103
  328.0 9.2 %convolution_bitcast_fusion = f32[8192,1,256]{0,2,1:T(8,128)} fusion(bf16[256,512]{1,0:T(8,128)(2,1)S(1)} %copy-done, bf16[8192,512]{0,1:T(8,128)(2,1)} %all-gather.2.cloned.1.call-done), kind=kOutput, calls=%fused_computation.47 | convolution fusion | flops 2147483648 | bytes 17039360 | tf_op jit(solution)/shard_map/dot_general | solution.py:17
  337.2 29.3 %pad_maximum_fusion = (f32[8192,2,256]{0,2,1:T(8,128)}, f32[8192,2,256]{0,2,1:T(8,128)}) fusion(f32[8192,1,256]{0,2,1:T(8,128)} %convolution_bitcast_fusion.1, f32[8192,1,256]{0,2,1:T(8,128)} %convolution_bitcast_fusion, f32[2,256]{1,0:T(2,128)S(1)} %get-tuple-element.92, f32[2,256]{1,0:T(2,128)S(1)} %get-tuple-element.94, ...), kind=kLoop, calls=%fused_computation.19 | loop fusion | flops 104857600 | bytes 67244032 | tf_op jit(solution)/shard_map/stack | solution.py:112
  366.5 8.7 %fusion.51 = (f32[8192,2]{0,1:T(2,128)}, f32[8192,2]{0,1:T(2,128)}) fusion(f32[8192,2,256]{0,2,1:T(8,128)} %get-tuple-element.75, f32[8192,2]{0,1:T(2,128)S(1)} %get-tuple-element.82, f32[8192,2]{0,1:T(2,128)S(1)} %get-tuple-element.81, f32[8192,512]{0,1:T(8,128)S(1)} %bitcast.218), kind=kLoop, calls=%fused_computation.119 | loop fusion | flops 20938752 | bytes 33816576 | tf_op jit(solution)/shard_map/reduce_sum | solution.py:119
  375.3 7.8 %fusion.27 = f32[256,512]{1,0:T(8,128)} fusion(bf16[8192,512]{0,1:T(8,128)(2,1)} %all-gather.2.cloned.1.call-done, bf16[8192,2,256]{0,2,1:T(8,128)(2,1)} %copy-done.4), kind=kOutput, calls=%fused_computation.71 | convolution fusion | flops 2147483648 | bytes 13107200 | tf_op jit(solution)/shard_map/dot_general | solution.py:17
  383.1 28.7 %fusion.50 = (f32[512]{0:T(512)S(1)}, f32[512]{0:T(512)S(1)}, f32[8192,512]{0,1:T(8,128)}) fusion(f32[8192,2]{0,1:T(2,128)S(1)} %get-tuple-element.82, f32[8192,512]{0,1:T(8,128)} %get-tuple-element.93, f32[8192,2]{0,1:T(2,128)S(1)} %get-tuple-element.81, f32[512]{0:T(512)S(1)} %bitcast.230, f32[512]{0:T(512)S(1)} %bitcast.228, ...), kind=kLoop, calls=%fused_computation.118 | loop fusion | flops 109050880 | bytes 50470912 | tf_op jit(solution)/shard_map/reduce_sum | solution.py:116
  413.5 12.9 %convert_reduce_fusion.1 = (f32[512]{0:T(512)S(1)}, bf16[8192,512]{0,1:T(8,128)(2,1)S(1)}) fusion(f32[8192,2]{0,1:T(2,128)S(1)} %multiply_bitcast_fusion, f32[8192,512]{0,1:T(8,128)} %get-tuple-element.93, f32[8192,2]{0,1:T(2,128)S(1)} %get-tuple-element.81, f32[8192,2]{0,1:T(2,128)S(1)} %multiply_bitcast_fusion.1, f32[8192,512]{0,1:T(8,128)} %get-tuple-element.71, ...), kind=kLoop, calls=%fused_computation.37 | loop fusion | flops 41942528 | bytes 42209280 | tf_op jit(solution)/shard_map/reduce_sum | solution.py:125
  432.4 9.7 %convolution_bitcast_fusion.3 = f32[512,512]{1,0:T(8,128)S(1)} fusion(bf16[8192,512]{0,1:T(8,128)(2,1)} %copy-done.2, bf16[8192,512]{1,0:T(8,128)(2,1)} %param.20), kind=kOutput, calls=%fused_computation.88 | convolution fusion | flops 4294967296 | bytes 17825792 | tf_op jit(solution)/shard_map/dot_general | solution.py:17
  443.7 10.3 %convolution_convert_fusion = bf16[8192,512]{1,0:T(8,128)(2,1)} fusion(bf16[8192,512]{0,1:T(8,128)(2,1)} %copy-done.2, bf16[614,512]{1,0:T(8,128)(2,1)S(1)} %copy-done.8), kind=kOutput, calls=%fused_computation.45 | convolution fusion | flops 4299161600 | bytes 17301504 | tf_op jit(solution)/shard_map/dot_general | solution.py:17
  453.9 11.8 %copy.49 = bf16[8192,512]{0,1:T(8,128)(2,1)} copy(bf16[8192,512]{1,0:T(8,128)(2,1)} %convolution_convert_fusion) | data formatting | bytes 16777216
  481.9 41.2 %all-reduce = (f32[1]{0:T(128)}, f32[1]{0:T(128)}, f32[80,96]{1,0:T(8,128)}) all-reduce(f32[1]{0:T(128)} %bitcast.30, f32[1]{0:T(128)} %bitcast.29, f32[80,96]{1,0:T(8,128)S(1)} %fusion.41), channel_id=1, replica_groups=mesh['dp'=8,'mp'=4] {'dp','mp'}, use_global_device_ids=true, to_apply=%region_19.20 | all-reduce | flops 7682 | bytes 61456 | tf_op jit(solution)/shard_map/psum | solution.py:139
  523.1 22.9 %all-reduce.1 = (f32[512]{0:T(512)S(1)}, f32[2,256]{1,0:T(2,128)S(1)}, f32[2,256]{1,0:T(2,128)S(1)}, f32[512]{0:T(512)}, f32[101]{0:T(128)}) all-reduce(f32[512]{0:T(512)S(1)} %get-tuple-element.72, f32[2,256]{1,0:T(2,128)S(1)} %reduce_sum.142, f32[2,256]{1,0:T(2,128)S(1)} %reduce_sum.144, ...), channel_id=1, replica_groups=mesh['dp'=8,'mp'=4] {'dp'}, use_global_device_ids=true, to_apply=%region_23.24 | all-reduce | flops 2149 | bytes 17192 | tf_op jit(solution)/shard_map/psum | solution.py:141
  552.2 64.2 %reduce-scatter.9.cloned.1.call-done = bf16[128,8192]{1,0:T(8,128)(2,1)} async-done(((bf16[512,8192]{1,0:T(8,128)(2,1)}), bf16[128,8192]{1,0:T(8,128)(2,1)}) %reduce-scatter.9.cloned.1.call-update) | async-done | bytes 2097168
  (135 shorter events, 74.2 us)
Async XLA Ops:
  7.2 95.6 %copy-start = (bf16[256,512]{1,0:T(8,128)(2,1)S(1)}, bf16[256,512]{1,0:T(8,128)(2,1)}, u32[]{:S(2)}) copy-start(bf16[256,512]{1,0:T(8,128)(2,1)} %param.36) | copy-start | bytes 786436
  7.2 76.7 %all-reduce.16.cloned.1.call-start = ((), (), s32[]{:S(2)}) async-start(), calls=%async_computation.8 | async-start | bytes 262144 | tf_op jit(solution)/shard_map/psum | solution.py:70
  29.6 20.2 %copy-start.26 = (f32[256]{0:T(256)S(1)}, f32[256]{0:T(256)}, u32[]{:S(2)}) copy-start(f32[256]{0:T(256)} %param.35) | copy-start | bytes 3076
  29.6 20.2 %copy-start.27 = (f32[256]{0:T(256)S(1)}, f32[256]{0:T(256)}, u32[]{:S(2)}) copy-start(f32[256]{0:T(256)} %param.31) | copy-start | bytes 3076
  29.7 20.2 %copy-start.28 = (f32[256]{0:T(256)S(1)}, f32[256]{0:T(256)}, u32[]{:S(2)}) copy-start(f32[256]{0:T(256)} %param.34) | copy-start | bytes 3076
  49.6 142.8 %reduce-scatter.7.cloned.1.call-start = ((), (), s32[]{:S(2)}) async-start(), calls=%async_computation.4 | async-start | bytes 10485760
  120.5 147.0 %all-reduce.10.cloned.1.call-start = ((), (), s32[]{:S(2)}) async-start(), calls=%async_computation.3 | async-start | bytes 6815744 | tf_op jit(solution)/shard_map/psum | solution.py:89
  123.5 75.3 %copy-start.6 = (bf16[8192,128]{0,1:T(8,128)(2,1)}, bf16[8192,128]{0,1:T(8,128)(2,1)S(1)}, u32[]{:S(2)}) copy-start(bf16[8192,128]{0,1:T(8,128)(2,1)S(1)} %copy.45) | copy-start | bytes 6291460
  124.3 68.1 %copy-start.24 = (f32[128]{0:T(128)}, f32[128]{0:T(128)S(1)}, u32[]{:S(2)}) copy-start(f32[128]{0:T(128)S(1)} %dynamic_slice.3) | copy-start | bytes 1540
  129.9 198.0 %all-gather.2.cloned.1.call-start = ((), (), s32[]{:S(2)}) async-start(), calls=%async_computation.2 | async-start | bytes 10485760 | tf_op jit(solution)/shard_map/all_gather | solution.py:103
  205.9 66.8 %copy-start.18 = (f32[8192]{0:T(1024)S(1)}, f32[8192]{0:T(1024)}, u32[]{:S(2)}) copy-start(f32[8192]{0:T(1024)} %param.26) | copy-start | bytes 98308
  205.9 66.8 %copy-start.19 = (s32[8192]{0:T(1024)S(1)}, s32[8192]{0:T(1024)}, u32[]{:S(2)}) copy-start(s32[8192]{0:T(1024)} %param.25) | copy-start | bytes 98308
  205.9 66.8 %copy-start.23 = (f32[101]{0:T(128)S(1)}, f32[101]{0:T(128)}, u32[]{:S(2)}) copy-start(f32[101]{0:T(128)} %param.39) | copy-start | bytes 1216
  205.9 70.8 %copy-start.15 = (bf16[256,101]{0,1:T(8,128)(2,1)S(1)}, bf16[256,101]{0,1:T(8,128)(2,1)}, u32[]{:S(2)}) copy-start(bf16[256,101]{0,1:T(8,128)(2,1)} %param.38) | copy-start | bytes 155140
  206.0 205.8 %all-reduce.14.cloned.1.call-start = ((), (), s32[]{:S(2)}) async-start(), calls=%async_computation.7 | async-start | bytes 262144 | tf_op jit(solution)/shard_map/psum | solution.py:118
  328.0 38.5 %slice-start = ((s8[16777216]{0:T(1024)(128)(4,1)}), s8[4194304]{0:T(1024)(128)(4,1)S(1)}, s32[]{:S(2)}) async-start(s8[16777216]{0:T(1024)(128)(4,1)} %bitcast.217), calls=%async_computation.9 | async-start | bytes 8388608
  337.2 29.3 %slice-start.1 = ((s8[16777216]{0:T(1024)(128)(4,1)}), s8[4194304]{0:T(1024)(128)(4,1)S(1)}, s32[]{:S(2)}) async-start(s8[16777216]{0:T(1024)(128)(4,1)} %bitcast.217), calls=%async_computation.10 | async-start | bytes 8388608
  337.2 29.3 %slice-start.2 = ((s8[16777216]{0:T(1024)(128)(4,1)}), s8[4194304]{0:T(1024)(128)(4,1)S(1)}, s32[]{:S(2)}) async-start(s8[16777216]{0:T(1024)(128)(4,1)} %bitcast.217), calls=%async_computation.11 | async-start | bytes 8388608
  337.2 29.3 %slice-start.3 = ((s8[16777216]{0:T(1024)(128)(4,1)}), s8[4194304]{0:T(1024)(128)(4,1)S(1)}, s32[]{:S(2)}) async-start(s8[16777216]{0:T(1024)(128)(4,1)} %bitcast.217), calls=%async_computation.12 | async-start | bytes 8388608
  375.2 174.5 %all-reduce.12.cloned.1.call-start = ((), (), s32[]{:S(2)}) async-start(), calls=%async_computation.6 | async-start | bytes 3784704 | tf_op jit(solution)/shard_map/psum | solution.py:141
  443.6 172.8 %reduce-scatter.9.cloned.1.call-start = ((), (), s32[]{:S(2)}) async-start(), calls=%async_computation.5 | async-start | bytes 10485760
  476.0 146.8 %copy-start.1 = (bf16[256,512]{1,0:T(8,128)(2,1)S(1)}, bf16[256,512]{1,0:T(8,128)(2,1)}, u32[]{:S(2)}) copy-start(bf16[256,512]{1,0:T(8,128)(2,1)} %param.36) | copy-start | bytes 786436
  549.7 71.7 %copy-start.13 = (f32[256,512]{1,0:T(8,128)S(1)}, f32[256,512]{1,0:T(8,128)}, u32[]{:S(2)}) copy-start(f32[256,512]{1,0:T(8,128)} %get-tuple-element.108) | copy-start | bytes 1572868
  549.7 72.5 %copy-start.20 = (f32[256,101]{0,1:T(8,128)S(1)}, f32[256,101]{0,1:T(8,128)}, u32[]{:S(2)}) copy-start(f32[256,101]{0,1:T(8,128)} %get-tuple-element.110) | copy-start | bytes 310276
  (21 other events, 188.5 us)
Sparse Core Ops, SparseCore 0:
  49.7 34.1 all-reduce.15
  120.6 71.7 reduce-scatter.6
  194.8 72.6 all-reduce.9
  269.5 58.3 all-gather.1
  375.3 31.5 all-reduce.13
  443.7 98.5 all-reduce.11
  544.9 71.4 reduce-scatter.8
where the time goes:
time: 637 us; the launch traced here: 630 us
  waiting for transfers between devices  263 us (41%)
  other arithmetic  136 us (21%)
  matrix products  102 us (16%)
  blocking collectives  64.2 us (10%)
  local copies, waits for them, and re-layouts  47.8 us (8%)
  between operations  15.8 us (2%)
    unnamed x9, waiting for transfers between devices  126 us
    dot_general x9, matrix products, contract(): lax.dot_general(left, right, (((left_dim,), (right_dim,)), ((), ())), pre...  68 us
    psum x1, waiting for transfers between devices, on_device(): logits = lax.psum(logit_part, 'mp') + rew_b2  59.5 us
    all_gather x1, waiting for transfers between devices, on_device(): d_full = lax.all_gather(d_share, 'mp', axis=1, tiled=True)  43.2 us
    unnamed x86, local copies, waits for them, and re-layouts  41.7 us
    psum x1, blocking collectives, on_device(): lax.psum((cons_part, rew_part, embed_part), ('dp', 'mp'))  41.2 us
    psum x1, waiting for transfers between devices, on_device(): lax.psum((jnp.sum(pre_act, axis=2).T, jnp.sum(pre_act * pre_act, axis=2)....  34 us
    another operation x1, other arithmetic, on_device(): d_hidden = jnp.stack([d_hid_dyn, d_hid_rew], axis=1)  29.3 us
  transfers between devices with their start and end apart: 7, of which 5 were waited for; matrix products, arithmetic and copies ran while one was open for 19% of the time, Pallas kernels for 0%

commit v1 on v0

--- a/solution.py
+++ b/solution.py
@@ -7,6 +7,19 @@
 GROUP = 8
 CONS_COEF = 20.0
 REW_COEF = 0.1
+
+
+def ring_gather(shard, axis, dim):
+    ways = lax.axis_size(axis)
+    up = [(d, (d + 1) % ways) for d in range(ways)]
+    down = [(d, (d - 1) % ways) for d in range(ways)]
+    earlier, later = ([shard], [shard])
+    for _ in range(ways // 2):
+        earlier.append(lax.ppermute(earlier[-1], axis, up))
+    for _ in range((ways - 1) // 2):
+        later.append(lax.ppermute(later[-1], axis, down))
+    line = jnp.concatenate([*earlier[::-1], *later[1:]], axis=dim)
+    return jnp.roll(line, (lax.axis_index(axis) - ways // 2) * shard.shape[dim], axis=dim)
 
 
 def mish_act(values):
@@ -100,7 +113,7 @@
     d_groups = (2.0 * CONS_COEF / total_rows * lat_error).reshape(groups.shape)
     d_lat = simplex * (d_groups - jnp.sum(simplex * d_groups, axis=-1, keepdims=True))
     d_share = d_lat.reshape(tok_rows, share_width).astype(jnp.bfloat16)
-    d_full = lax.all_gather(d_share, "mp", axis=1, tiled=True)
+    d_full = ring_gather(d_share, "mp", 1)
     d_logits = (REW_COEF / total_rows * (jnp.exp(log_probs) - target)).astype(jnp.bfloat16)
     grad_w2_dyn = contract(hidden_dyn, d_full, 0, 0)
     grad_b2_dyn = jnp.sum(d_full.astype(jnp.float32), axis=0)

time: 637 us -> 680 us (1.068)
  local copies, waits for them, and re-layouts: 47.8 us -> 67.4 us
  waiting for transfers between devices: 263 us -> 279 us
  starting transfers between devices: 1.22 us -> 13.7 us
    ppermute x0 -> x3, waiting for transfers between devices: none -> 65.5 us  [the longest x2 49.7 us: ring_gather(): earlier.append(lax.ppermute(earlier[-1], axis, up))]
    all_gather x1 -> x0, waiting for transfers between devices: 43.2 us -> none  [on_device(): d_full = lax.all_gather(d_share, 'mp', axis=1, tiled=True)]
    unnamed x86 -> x95, local copies, waits for them, and re-layouts: 41.7 us -> 59.7 us
    ppermute x0 -> x3, starting transfers between devices: none -> 13.1 us  [the longest x2 13.1 us: ring_gather(): earlier.append(lax.ppermute(earlier[-1], axis, up))]
    psum x1, waiting for transfers between devices: 59.5 us -> 48.4 us  [on_device(): logits = lax.psum(logit_part, 'mp') + rew_b2]
    unnamed x9 -> x8, waiting for transfers between devices: 126 us -> 132 us
  transfers between devices with their start and end apart: 7 -> 9, of which waited for: 5 -> 6; matrix products, arithmetic and copies ran while one was open for 19% -> 17% of each run, Pallas kernels for 0% -> 0%
where the time goes in v1:
time: 680 us; the launch traced here: 673 us
  waiting for transfers between devices  279 us (41%)
  other arithmetic  134 us (20%)
  matrix products  97.5 us (14%)
  local copies, waits for them, and re-layouts  67.4 us (10%)
  blocking collectives  65.8 us (10%)
  between operations  15.6 us (2%)
  starting transfers between devices  13.7 us (2%)
    unnamed x8, waiting for transfers between devices  132 us
    dot_general x9, matrix products, contract(): lax.dot_general(left, right, (((left_dim,), (right_dim,)), ((), ())), pre...  66.6 us
    unnamed x95, local copies, waits for them, and re-layouts  59.7 us
    ppermute x2, waiting for transfers between devices, ring_gather(): earlier.append(lax.ppermute(earlier[-1], axis, up))  49.7 us
    psum x1, waiting for transfers between devices, on_device(): logits = lax.psum(logit_part, 'mp') + rew_b2  48.4 us
    psum x1, blocking collectives, on_device(): lax.psum((cons_part, rew_part, embed_part), ('dp', 'mp'))  43 us
    psum x1, waiting for transfers between devices, on_device(): lax.psum((jnp.sum(pre_act, axis=2).T, jnp.sum(pre_act * pre_act, axis=2)....  33.9 us
    reduce_sum x1, other arithmetic, on_device(): grad_shift = jnp.sum(d_normed, axis=0)  28.9 us
  transfers between devices with their start and end apart: 9, of which 6 were waited for; matrix products, arithmetic and copies ran while one was open for 17% of the time, Pallas kernels for 0%

profile of v1, /device:TPU:0, one launch (start us, length us, event | category | flops | bytes accessed | tf_op | source)
XLA Modules:
  0.0 673.3 jit_solution(2645775570115903853)
XLA Ops:
  10.0 11.8 %fusion.41 = f32[512,8192]{1,0:T(8,128)} fusion(bf16[8192,512]{1,0:T(8,128)(2,1)} %param.20, bf16[614,512]{1,0:T(8,128)(2,1)S(1)} %constant_dynamic-update-slice_fusion), kind=kOutput, calls=%fused_computation.97 | convolution fusion | flops 4294967296 | bytes 25690112 | tf_op jit(solution)/shard_map/dot_general | solution.py:77
  21.8 7.2 %fusion.35 = f32[8192,512]{0,1:T(8,128)} fusion(bf16[80,96]{1,0:T(8,128)(2,1)S(1)} %copy-done.19, s32[8192]{0:T(1024)S(1)} %copy-done.16, bf16[614,512]{1,0:T(8,128)(2,1)S(1)} %constant_dynamic-update-slice_fusion), kind=kOutput, calls=%fused_computation.89 | convolution fusion | flops 932577280 | bytes 16928768 | tf_op jit(solution)/shard_map/dot_general | solution.py:79
  29.6 19.9 %bitcast_reduce_fusion = (f32[8192,2]{0,1:T(2,128)}, f32[8192,2]{0,1:T(2,128)}, f32[8192,512]{0,1:T(8,128)}) fusion(f32[512]{0:T(512)S(1)} %pad_maximum_fusion.2, f32[8192,512]{0,1:T(8,128)} %fusion.35, bf16[6,8192]{1,0:T(8,128)(2,1)S(1)} %fusion.23, bf16[614,512]{1,0:T(8,128)(2,1)S(1)} %constant_dynamic-update-slice_fusion, f32[512,8192]{1,0:T(8,128)} %fusion.41), kind=kOutput, calls=%fused_computation.29 | convolution fusion | flops 75464704 | bytes 50604032 | tf_op jit(solution)/shard_map/dot_general | solution.py:30
  50.0 33.9 %all-reduce.16.cloned.1.call-done = (f32[2,8192]{1,0:T(2,128)}, f32[2,8192]{1,0:T(2,128)}) async-done(((f32[2,8192]{1,0:T(2,128)}, f32[2,8192]{1,0:T(2,128)}), (f32[2,8192]{1,0:T(2,128)}, f32[2,8192]{1,0:T(2,128)})) %all-reduce.16.cloned.1.call-update) | async-done | bytes 131088 | tf_op jit(solution)/shard_map/psum | solution.py:83
  84.8 14.7 %fusion.17 = bf16[8192,2,256]{0,2,1:T(8,128)(2,1)S(1)} fusion(f32[8192,512]{0,1:T(8,128)} %get-tuple-element.93, f32[2,256]{1,0:T(2,128)S(1)} %get-tuple-element.92, f32[2,256]{1,0:T(2,128)S(1)} %get-tuple-element.94, f32[8192,2]{0,1:T(2,128)S(1)} %get-tuple-element.82, f32[8192,2]{0,1:T(2,128)S(1)} %get-tuple-element.81), kind=kLoop, calls=%fused_computation.41 | loop fusion | flops 50331648 | bytes 25300992 | tf_op jit(solution)/shard_map/convert_element_type | solution.py:93
  108.4 11.4 %copy.47 = bf16[8192,512]{0,1:T(8,128)(2,1)} copy(bf16[8192,512]{1,0:T(8,128)(2,1)} %convolution_convert_fusion.1) | data formatting | bytes 16777216
  125.0 66.7 %reduce-scatter.7.cloned.1.call-done = bf16[128,8192]{1,0:T(8,128)(2,1)} async-done(((bf16[512,8192]{1,0:T(8,128)(2,1)}), bf16[128,8192]{1,0:T(8,128)(2,1)}) %reduce-scatter.7.cloned.1.call-update) | async-done | bytes 2097168
  198.3 7.5 %fusion.21 = bf16[8192,128]{0,1:T(8,128)(2,1)S(1)} fusion(bf16[8192,128]{0,1:T(8,128)(2,1)} %copy.45, bf16[128,8192]{1,0:T(8,128)(2,1)} %reduce-scatter.7.cloned.1.call-done, f32[8192,16]{0,1:T(8,128)S(1)} %fusion.29, f32[8192,16]{0,1:T(8,128)S(1)} %bitcast_reduce_fusion.1, f32[128]{0:T(128)} %copy-done.22), kind=kOutput, calls=%fused_computation.52 | output fusion | flops 21102600 | bytes 7340544 | tf_op jit(solution)/shard_map/sub | solution.py:114
  205.8 13.1 %collective-permute-start = (bf16[8192,128]{0,1:T(8,128)(2,1)S(1)}, bf16[8192,128]{0,1:T(8,128)(2,1)}, u32[]{:S(2)}, u32[]{:S(2)}) collective-permute-start(bf16[8192,128]{0,1:T(8,128)(2,1)S(1)} %fusion.21), channel_id=1, source_target_pairs={{0,1},{1,2},{2,3},{3,0},{4,5},{5,6},{6,7},{7,4},{8,9},{9,10},{10,1... | collective-permute-start | bytes 6291464 | tf_op jit(solution)/shard_map/ppermute | solution.py:18
  222.1 49.7 %collective-permute-done = bf16[8192,128]{0,1:T(8,128)(2,1)} collective-permute-done((bf16[8192,128]{0,1:T(8,128)(2,1)S(1)}, bf16[8192,128]{0,1:T(8,128)(2,1)}, u32[]{:S(2)}, u32[]{:S(2)}) %collective-permute-start) | collective-permute-done | bytes 2097184 | tf_op jit(solution)/shard_map/ppermute | solution.py:18
  274.5 48.4 %all-reduce.10.cloned.1.call-done = f32[8192,101]{0,1:T(8,128)} async-done(((f32[8192,101]{0,1:T(8,128)}), f32[8192,101]{0,1:T(8,128)}) %all-reduce.10.cloned.1.call-update) | async-done | bytes 3309584 | tf_op jit(solution)/shard_map/psum | solution.py:102
  346.1 15.8 %collective-permute-done.2 = bf16[8192,128]{0,1:T(8,128)(2,1)S(1)} collective-permute-done((bf16[8192,128]{0,1:T(8,128)(2,1)S(1)}, bf16[8192,128]{0,1:T(8,128)(2,1)S(1)}, u32[]{:S(2)}, u32[]{:S(2)}) %collective-permute-start.2) | collective-permute-done | bytes 2097184 | tf_op jit(solution)/shard_map/ppermute | solution.py:20
  372.9 9.1 %convolution_bitcast_fusion = f32[8192,1,256]{0,2,1:T(8,128)} fusion(bf16[256,512]{1,0:T(8,128)(2,1)S(1)} %copy-done, bf16[8192,1024]{0,1:T(8,128)(2,1)} %constant_dynamic-update-slice_fusion.2, s32[]{:T(128)S(6)} %select_n.55), kind=kOutput, calls=%fused_computation.47 | convolution fusion | flops 2147483648 | bytes 17039364 | tf_op jit(solution)/shard_map/dot_general | solution.py:30
  382.0 25.9 %pad_maximum_fusion = (f32[8192,2,256]{0,2,1:T(8,128)}, f32[8192,2,256]{0,2,1:T(8,128)}) fusion(f32[8192,1,256]{0,2,1:T(8,128)} %convolution_bitcast_fusion.1, f32[8192,1,256]{0,2,1:T(8,128)} %convolution_bitcast_fusion, f32[2,256]{1,0:T(2,128)S(1)} %get-tuple-element.92, f32[2,256]{1,0:T(2,128)S(1)} %get-tuple-element.94, ...), kind=kLoop, calls=%fused_computation.19 | loop fusion | flops 104857600 | bytes 67244032 | tf_op jit(solution)/shard_map/stack | solution.py:125
  407.9 8.7 %fusion.55 = (f32[8192,2]{0,1:T(2,128)}, f32[8192,2]{0,1:T(2,128)}) fusion(f32[8192,2,256]{0,2,1:T(8,128)} %get-tuple-element.75, f32[8192,2]{0,1:T(2,128)S(1)} %get-tuple-element.82, f32[8192,2]{0,1:T(2,128)S(1)} %get-tuple-element.81, f32[8192,512]{0,1:T(8,128)S(1)} %bitcast.216), kind=kLoop, calls=%fused_computation.131 | loop fusion | flops 20938752 | bytes 33816576 | tf_op jit(solution)/shard_map/reduce_sum | solution.py:132
  416.7 7.8 %fusion.24 = f32[256,512]{1,0:T(8,128)} fusion(bf16[8192,1024]{0,1:T(8,128)(2,1)} %constant_dynamic-update-slice_fusion.2, s32[]{:T(128)S(6)} %select_n.55, bf16[8192,2,256]{0,2,1:T(8,128)(2,1)} %copy-done.4), kind=kOutput, calls=%fused_computation.57 | convolution fusion | flops 2147483648 | bytes 13107204 | tf_op jit(solution)/shard_map/dot_general | solution.py:30
  424.5 28.9 %fusion.54 = (f32[512]{0:T(512)S(1)}, f32[512]{0:T(512)S(1)}, f32[8192,512]{0,1:T(8,128)}) fusion(f32[8192,2]{0,1:T(2,128)S(1)} %get-tuple-element.82, f32[8192,512]{0,1:T(8,128)} %get-tuple-element.93, f32[8192,2]{0,1:T(2,128)S(1)} %get-tuple-element.81, f32[512]{0:T(512)S(1)} %bitcast.230, f32[512]{0:T(512)S(1)} %bitcast.228, ...), kind=kLoop, calls=%fused_computation.130 | loop fusion | flops 109050880 | bytes 50470912 | tf_op jit(solution)/shard_map/reduce_sum | solution.py:129
  455.2 12.9 %convert_reduce_fusion.1 = (f32[512]{0:T(512)S(1)}, bf16[8192,512]{0,1:T(8,128)(2,1)S(1)}) fusion(f32[8192,2]{0,1:T(2,128)S(1)} %multiply_bitcast_fusion, f32[8192,512]{0,1:T(8,128)} %get-tuple-element.93, f32[8192,2]{0,1:T(2,128)S(1)} %get-tuple-element.81, f32[8192,2]{0,1:T(2,128)S(1)} %multiply_bitcast_fusion.1, f32[8192,512]{0,1:T(8,128)} %get-tuple-element.71, ...), kind=kLoop, calls=%fused_computation.37 | loop fusion | flops 41942528 | bytes 42209280 | tf_op jit(solution)/shard_map/reduce_sum | solution.py:138
  474.0 9.7 %convolution_bitcast_fusion.3 = f32[512,512]{1,0:T(8,128)S(1)} fusion(bf16[8192,512]{0,1:T(8,128)(2,1)} %copy-done.2, bf16[8192,512]{1,0:T(8,128)(2,1)} %param.20), kind=kOutput, calls=%fused_computation.90 | convolution fusion | flops 4294967296 | bytes 17825792 | tf_op jit(solution)/shard_map/dot_general | solution.py:30
  485.3 10.3 %convolution_convert_fusion = bf16[8192,512]{1,0:T(8,128)(2,1)} fusion(bf16[8192,512]{0,1:T(8,128)(2,1)} %copy-done.2, bf16[614,512]{1,0:T(8,128)(2,1)S(1)} %copy-done.8), kind=kOutput, calls=%fused_computation.45 | convolution fusion | flops 4299161600 | bytes 17301504 | tf_op jit(solution)/shard_map/dot_general | solution.py:30
  495.6 11.3 %copy.49 = bf16[8192,512]{0,1:T(8,128)(2,1)} copy(bf16[8192,512]{1,0:T(8,128)(2,1)} %convolution_convert_fusion) | data formatting | bytes 16777216
  522.9 43.0 %all-reduce = (f32[1]{0:T(128)}, f32[1]{0:T(128)}, f32[80,96]{1,0:T(8,128)}) all-reduce(f32[1]{0:T(128)} %bitcast.30, f32[1]{0:T(128)} %bitcast.29, f32[80,96]{1,0:T(8,128)S(1)} %fusion.43), channel_id=1, replica_groups=mesh['dp'=8,'mp'=4] {'dp','mp'}, use_global_device_ids=true, to_apply=%region_19.20 | all-reduce | flops 7682 | bytes 61456 | tf_op jit(solution)/shard_map/psum | solution.py:152
  565.9 22.8 %all-reduce.1 = (f32[512]{0:T(512)S(1)}, f32[2,256]{1,0:T(2,128)S(1)}, f32[2,256]{1,0:T(2,128)S(1)}, f32[512]{0:T(512)}, f32[101]{0:T(128)}) all-reduce(f32[512]{0:T(512)S(1)} %get-tuple-element.72, f32[2,256]{1,0:T(2,128)S(1)} %reduce_sum.142, f32[2,256]{1,0:T(2,128)S(1)} %reduce_sum.144, ...), channel_id=1, replica_groups=mesh['dp'=8,'mp'=4] {'dp'}, use_global_device_ids=true, to_apply=%region_23.24 | all-reduce | flops 2149 | bytes 17192 | tf_op jit(solution)/shard_map/psum | solution.py:154
  595.0 64.9 %reduce-scatter.9.cloned.1.call-done = bf16[128,8192]{1,0:T(8,128)(2,1)} async-done(((bf16[512,8192]{1,0:T(8,128)(2,1)}), bf16[128,8192]{1,0:T(8,128)(2,1)}) %reduce-scatter.9.cloned.1.call-update) | async-done | bytes 2097168
  (149 shorter events, 102.3 us)
Async XLA Ops:
  7.2 95.6 %copy-start = (bf16[256,512]{1,0:T(8,128)(2,1)S(1)}, bf16[256,512]{1,0:T(8,128)(2,1)}, u32[]{:S(2)}) copy-start(bf16[256,512]{1,0:T(8,128)(2,1)} %param.36) | copy-start | bytes 786436
  7.2 76.6 %all-reduce.16.cloned.1.call-start = ((), (), s32[]{:S(2)}) async-start(), calls=%async_computation.7 | async-start | bytes 262144 | tf_op jit(solution)/shard_map/psum | solution.py:83
  10.0 19.6 %copy-start.7 = (bf16[614,512]{1,0:T(8,128)(2,1)}, bf16[614,512]{1,0:T(8,128)(2,1)S(1)}, u32[]{:S(2)}) copy-start(bf16[614,512]{1,0:T(8,128)(2,1)S(1)} %constant_dynamic-update-slice_fusion) | copy-start | bytes 1886212
  29.5 19.9 %copy-start.11 = (bf16[6,8192]{1,0:T(8,128)(2,1)}, bf16[6,8192]{1,0:T(8,128)(2,1)S(1)}, u32[]{:S(2)}) copy-start(bf16[6,8192]{1,0:T(8,128)(2,1)S(1)} %fusion.23) | copy-start | bytes 294916
  29.6 20.4 %copy-start.25 = (f32[256]{0:T(256)S(1)}, f32[256]{0:T(256)}, u32[]{:S(2)}) copy-start(f32[256]{0:T(256)} %param.35) | copy-start | bytes 3076
  29.6 20.4 %copy-start.26 = (f32[256]{0:T(256)S(1)}, f32[256]{0:T(256)}, u32[]{:S(2)}) copy-start(f32[256]{0:T(256)} %param.31) | copy-start | bytes 3076
  29.6 20.4 %copy-start.27 = (f32[256]{0:T(256)S(1)}, f32[256]{0:T(256)}, u32[]{:S(2)}) copy-start(f32[256]{0:T(256)} %param.34) | copy-start | bytes 3076
  29.6 20.4 %copy-start.28 = (f32[256]{0:T(256)S(1)}, f32[256]{0:T(256)}, u32[]{:S(2)}) copy-start(f32[256]{0:T(256)} %param.30) | copy-start | bytes 3076
  49.5 142.2 %reduce-scatter.7.cloned.1.call-start = ((), (), s32[]{:S(2)}) async-start(), calls=%async_computation.3 | async-start | bytes 10485760
  119.8 203.1 %all-reduce.10.cloned.1.call-start = ((), (), s32[]{:S(2)}) async-start(), calls=%async_computation.2 | async-start | bytes 6815744 | tf_op jit(solution)/shard_map/psum | solution.py:102
  125.0 69.7 %copy-start.22 = (f32[128]{0:T(128)}, f32[128]{0:T(128)S(1)}, u32[]{:S(2)}) copy-start(f32[128]{0:T(128)S(1)} %dynamic_slice.7) | copy-start | bytes 1540
  194.8 24.1 %slice-start.4 = ((s8[8388608]{0:T(1024)(128)(4,1)}), s8[4194304]{0:T(1024)(128)(4,1)S(1)}, s32[]{:S(2)}) async-start(s8[8388608]{0:T(1024)(128)(4,1)} %bitcast.219), calls=%async_computation.12 | async-start | bytes 8388608
  198.3 20.6 %slice-start.5 = ((s8[8388608]{0:T(1024)(128)(4,1)}), s8[4194304]{0:T(1024)(128)(4,1)S(1)}, s32[]{:S(2)}) async-start(s8[8388608]{0:T(1024)(128)(4,1)} %bitcast.219), calls=%async_computation.13 | async-start | bytes 8388608
  198.3 20.6 %copy-start.14 = (bf16[256,101]{0,1:T(8,128)(2,1)S(1)}, bf16[256,101]{0,1:T(8,128)(2,1)}, u32[]{:S(2)}) copy-start(bf16[256,101]{0,1:T(8,128)(2,1)} %param.38) | copy-start | bytes 155140
  205.8 66.0 %collective-permute-start = (bf16[8192,128]{0,1:T(8,128)(2,1)S(1)}, bf16[8192,128]{0,1:T(8,128)(2,1)}, u32[]{:S(2)}, u32[]{:S(2)}) collective-permute-start(bf16[8192,128]{0,1:T(8,128)(2,1)S(1)} %fusion.21), channel_id=1, source_target_pairs={{0,1},{1,2},{2,3},{3,0},{4,5},{5,6},{6,7},{7,4},{8,9},{9,10},{10,1... | collective-permute-start | bytes 6291464 | tf_op jit(solution)/shard_map/ppermute | solution.py:18
  221.4 232.0 %all-reduce.14.cloned.1.call-start = ((), (), s32[]{:S(2)}) async-start(), calls=%async_computation.6 | async-start | bytes 262144 | tf_op jit(solution)/shard_map/psum | solution.py:131
  271.8 66.7 %collective-permute-start.1 = (bf16[8192,128]{0,1:T(8,128)(2,1)}, bf16[8192,128]{0,1:T(8,128)(2,1)}, u32[]{:S(2)}, u32[]{:S(2)}) collective-permute-start(bf16[8192,128]{0,1:T(8,128)(2,1)} %collective-permute-done), channel_id=1, source_target_pairs={{0,1},{1,2},{2,3},{3,0},{4,5},{5,6},{6,7},{7,4},{8,9},{9,10},{10,1... | collective-permute-start | bytes 6291464 | tf_op jit(solution)/shard_map/ppermute | solution.py:18
  338.4 23.6 %collective-permute-start.2 = (bf16[8192,128]{0,1:T(8,128)(2,1)S(1)}, bf16[8192,128]{0,1:T(8,128)(2,1)S(1)}, u32[]{:S(2)}, u32[]{:S(2)}) collective-permute-start(bf16[8192,128]{0,1:T(8,128)(2,1)S(1)} %fusion.21), channel_id=1, source_target_pairs={{0,3},{1,0},{2,1},{3,2},{4,7},{5,4},{6,5},{7,6},{8,11},{9,8},{10,9... | collective-permute-start | bytes 6291464 | tf_op jit(solution)/shard_map/ppermute | solution.py:20
  416.7 175.7 %all-reduce.12.cloned.1.call-start = ((), (), s32[]{:S(2)}) async-start(), calls=%async_computation.5 | async-start | bytes 3784704 | tf_op jit(solution)/shard_map/psum | solution.py:154
  485.2 174.7 %reduce-scatter.9.cloned.1.call-start = ((), (), s32[]{:S(2)}) async-start(), calls=%async_computation.4 | async-start | bytes 10485760
  508.5 57.4 %copy-start.24 = (f32[101]{0:T(128)S(1)}, f32[101]{0:T(128)}, u32[]{:S(2)}) copy-start(f32[101]{0:T(128)} %get-tuple-element.69) | copy-start | bytes 1216
  517.2 149.1 %copy-start.1 = (bf16[256,512]{1,0:T(8,128)(2,1)S(1)}, bf16[256,512]{1,0:T(8,128)(2,1)}, u32[]{:S(2)}) copy-start(bf16[256,512]{1,0:T(8,128)(2,1)} %param.36) | copy-start | bytes 786436
  592.3 72.5 %copy-start.13 = (f32[256,512]{1,0:T(8,128)S(1)}, f32[256,512]{1,0:T(8,128)}, u32[]{:S(2)}) copy-start(f32[256,512]{1,0:T(8,128)} %get-tuple-element.108) | copy-start | bytes 1572868
  592.3 73.3 %copy-start.18 = (f32[256,101]{0,1:T(8,128)S(1)}, f32[256,101]{0,1:T(8,128)}, u32[]{:S(2)}) copy-start(f32[256,101]{0,1:T(8,128)} %get-tuple-element.110) | copy-start | bytes 310276
  (24 other events, 188.4 us)
Sparse Core Ops, SparseCore 0:
  49.6 34.1 all-reduce.15
  120.0 71.7 reduce-scatter.6
  221.6 101.3 all-reduce.9
  416.8 33.1 all-reduce.13
  485.3 100.8 all-reduce.11
  588.7 71.1 reduce-scatter.8
